TPU v7x, 256 devices: a whole 4x4x8 slice. The times are simulated.
256 devices in a mesh: section: 2 (over x_hi), fsdp: 64 (over y, z, x_lo), dp: 2 (over core).
Axes of the slice: x: 4 (x_hi: 2, x_lo: 2; x = x_hi * 2 + x_lo), y: 4, z: 8, core: 2. Of those that a mesh axis runs over, the one named last changes fastest.
Arguments:
- hidden: bfloat16 [4, 512, 8192], P(('section', 'dp'), 'fsdp'), may hold values from -7 to 7
- cotangent: bfloat16 [4, 512, 8192], P(('section', 'dp'), None, 'fsdp'), may hold values from -6 to 6
- seg_ids: int32 [4, 512], P(('section', 'dp')), may hold values from 0 to 8, as said below
- advantage: float32 [4, 8], P(('section', 'dp')), may hold values from -4 to 4
- w_query: bfloat16 [8192, 8192], P('fsdp'), may hold values from -6 to 6
- w_key: bfloat16 [8192, 1024], P('fsdp'), may hold values from -6 to 6
- w_value: bfloat16 [8192, 1024], P('fsdp'), may hold values from -6 to 6
Outputs:
- rollout_query: bfloat16 [8192, 8192], P(None, 'fsdp')
- rollout_key: bfloat16 [8192, 8192], P(None, 'fsdp')
- rollout_value: bfloat16 [8192, 8192], P(None, 'fsdp')
Inputs may be any that keep to these rules, and one draw needn't show every extreme that they name: `seg_ids`: in each block ids never fall; each id below 8 covers 1 to 64 positions, one of them exactly 64, and every id below 8 appears; id 8 marks padding at the block's end.
All inputs are finite; a program needn't handle non-finite values.
Results may differ from a plain program's by a relative error of at most 0.015.
The roundings to bfloat16 on the way count: a program that leaves them out, or rounds other values in their place, can miss the bound.
Values may be sent and summed in bfloat16 or wider, within the bound.
No kernel may reach another device: no remote copies, remote signals or barrier semaphores. Data moves between devices by JAX's collectives and lax.ppermute only.
A program may use at most 64 MiB of HBM per device.

v0:
```python
import jax
import jax.numpy as jnp
from jax import lax
from jax.sharding import PartitionSpec as P

D = 8192
H = 64
KVH = 8
HD = 128
RESP = 8


step_rate = 200.0
rope_base = 1000000.0
norm_eps = 1e-06
masked_score = -1e30


def rotate(field, cosine_table, sine_table):
    half_width = field.shape[-1] // 2
    lead_half = field[..., :half_width]
    tail_half = field[..., half_width:]
    return jnp.concatenate(
        [
            lead_half * cosine_table - tail_half * sine_table,
            tail_half * cosine_table + lead_half * sine_table,
        ],
        -1,
    )


def unrotate(field, cosine_table, sine_table):
    half_width = field.shape[-1] // 2
    lead_half = field[..., :half_width]
    tail_half = field[..., half_width:]
    return jnp.concatenate(
        [
            lead_half * cosine_table + tail_half * sine_table,
            tail_half * cosine_table - lead_half * sine_table,
        ],
        -1,
    )


def angles(seg_row):
    span_count = seg_row.shape[0]
    earlier = jnp.sum((seg_row[None, :] < seg_row[:, None]).astype(jnp.int32), axis=1)
    positions = jnp.arange(span_count, dtype=jnp.int32) - earlier
    frequency = rope_base ** (-jnp.arange(HD // 2, dtype=jnp.float32) * 2.0 / HD)
    phase_grid = positions.astype(jnp.float32)[:, None] * frequency[None, :]
    return (jnp.cos(phase_grid)[:, None, :], jnp.sin(phase_grid)[:, None, :])


def token_weights(seg_row, advantage_row):
    id_range = jnp.arange(RESP + 1, dtype=jnp.int32)
    onehot = (seg_row[:, None] == id_range[None, :]).astype(jnp.float32)
    counts = jnp.sum(onehot, axis=0)[:RESP]
    per_token = -advantage_row / counts
    return jnp.sum(onehot[:, :RESP] * per_token[None, :], axis=1)


def attend_back(q_rot, k_rot, v_bf, grad_context, allowed):
    score_scale = HD ** (-0.5)
    scores = (
        jnp.einsum("tkjqd,ukd->kjqtu", q_rot, k_rot, preferred_element_type=jnp.float32)
        * score_scale
    )
    scores = jnp.where(allowed, scores, masked_score)
    row_top = jnp.max(scores, axis=-1, keepdims=True)
    exponent = jnp.exp(scores - row_top)
    attention = exponent / jnp.sum(exponent, axis=-1, keepdims=True)
    attention_bf = attention.astype(jnp.bfloat16)
    grad_prob = jnp.einsum(
        "tkjqd,ukd->kjqtu", grad_context, v_bf, preferred_element_type=jnp.float32
    )
    inner_sum = jnp.sum(attention * grad_prob, axis=-1, keepdims=True)
    dscore = (attention * (grad_prob - inner_sum)).astype(jnp.bfloat16)
    grad_query = (
        jnp.einsum("kjqtu,ukd->tkjqd", dscore, k_rot, preferred_element_type=jnp.float32)
        * score_scale
    )
    grad_key = (
        jnp.einsum("kjqtu,tkjqd->ukjd", dscore, q_rot, preferred_element_type=jnp.float32)
        * score_scale
    )
    grad_value = jnp.einsum(
        "kjqtu,tkjqd->ukjd", attention_bf, grad_context, preferred_element_type=jnp.float32
    )
    return (grad_query, grad_key, grad_value)


def local(hidden, cotangent, seg_ids, advantage, w_query, w_key, w_value):
    fsdp_size = lax.axis_size("fsdp")
    share_count = max(1, fsdp_size // KVH)
    kv_local = max(1, KVH // fsdp_size)
    heads_local = H // fsdp_size
    per_copy = heads_local // kv_local
    inv_width = D ** (-0.5)

    def to_rollout(q_part, k_part, v_part):
        width_rows = q_part.shape[0]
        k_wide = jnp.repeat(k_part.reshape(width_rows, KVH, HD), share_count, axis=1).reshape(
            width_rows, KVH * share_count * HD
        )
        v_wide = jnp.repeat(v_part.reshape(width_rows, KVH, HD), share_count, axis=1).reshape(
            width_rows, KVH * share_count * HD
        )
        return (
            lax.all_to_all(q_part, "fsdp", split_axis=1, concat_axis=0, tiled=True),
            lax.all_to_all(k_wide, "fsdp", split_axis=1, concat_axis=0, tiled=True),
            lax.all_to_all(v_wide, "fsdp", split_axis=1, concat_axis=0, tiled=True),
        )

    gathered = lax.all_gather(hidden, "fsdp", axis=1, tiled=True)
    q_cols, k_cols, v_cols = to_rollout(w_query, w_key, w_value)
    token_rows = gathered[0].astype(jnp.float32)
    block_len = token_rows.shape[0]
    normed = (
        token_rows * lax.rsqrt(jnp.mean(token_rows * token_rows, axis=-1, keepdims=True) + norm_eps)
    ).astype(jnp.bfloat16)
    queries = jnp.dot(normed, q_cols, preferred_element_type=jnp.float32) * inv_width
    key_proj = jnp.dot(normed, k_cols, preferred_element_type=jnp.float32) * inv_width
    value_proj = jnp.dot(normed, v_cols, preferred_element_type=jnp.float32) * inv_width
    seg_row = seg_ids[0]
    cosine_table, sine_table = angles(seg_row)
    q_rot = rotate(queries.reshape(block_len, heads_local, HD), cosine_table, sine_table).astype(
        jnp.bfloat16
    )
    k_rot = rotate(key_proj.reshape(block_len, kv_local, HD), cosine_table, sine_table).astype(
        jnp.bfloat16
    )
    v_bf = value_proj.astype(jnp.bfloat16).reshape(block_len, kv_local, HD)
    weight_row = token_weights(seg_row, advantage[0])
    grad_context = (cotangent[0].astype(jnp.float32) * weight_row[:, None]).astype(jnp.bfloat16)
    place = jnp.arange(block_len, dtype=jnp.int32)
    allowed = (seg_row[:, None] == seg_row[None, :]) & (place[None, :] <= place[:, None])
    grad_query, grad_key, grad_value = attend_back(
        q_rot.reshape(block_len, kv_local, 1, per_copy, HD),
        k_rot,
        v_bf,
        grad_context.reshape(block_len, kv_local, 1, per_copy, HD),
        allowed,
    )
    grad_query = unrotate(grad_query.reshape(block_len, heads_local, HD), cosine_table, sine_table)
    grad_key = unrotate(grad_key.reshape(block_len, kv_local, HD), cosine_table, sine_table)
    scaled_q = (grad_query.reshape(block_len, heads_local * HD) * inv_width).astype(jnp.bfloat16)
    scaled_k = (grad_key.reshape(block_len, kv_local * HD) * inv_width).astype(jnp.bfloat16)
    scaled_v = (grad_value.reshape(block_len, kv_local * HD) * inv_width).astype(jnp.bfloat16)
    contract = (((0,), (0,)), ((), ()))
    part_q = lax.dot_general(normed, scaled_q, contract, preferred_element_type=jnp.float32).astype(
        jnp.bfloat16
    )
    part_k = lax.dot_general(normed, scaled_k, contract, preferred_element_type=jnp.float32).astype(
        jnp.bfloat16
    )
    part_v = lax.dot_general(normed, scaled_v, contract, preferred_element_type=jnp.float32).astype(
        jnp.bfloat16
    )
    back_q, back_k, back_v = (
        lax.all_to_all(part_q, "fsdp", split_axis=0, concat_axis=1, tiled=True),
        lax.all_to_all(part_k, "fsdp", split_axis=0, concat_axis=1, tiled=True),
        lax.all_to_all(part_v, "fsdp", split_axis=0, concat_axis=1, tiled=True),
    )
    width_rows = back_q.shape[0]
    sum_k = jnp.sum(
        back_k.astype(jnp.float32).reshape(width_rows, KVH, share_count, HD), axis=2
    ).reshape(width_rows, KVH * HD)
    sum_v = jnp.sum(
        back_v.astype(jnp.float32).reshape(width_rows, KVH, share_count, HD), axis=2
    ).reshape(width_rows, KVH * HD)
    query_sum = back_q.astype(jnp.float32)
    total_q, total_k, total_v = lax.psum((query_sum, sum_k, sum_v), ("section", "dp"))
    new_q = (w_query.astype(jnp.float32) - step_rate * total_q).astype(jnp.bfloat16)
    new_k = (w_key.astype(jnp.float32) - step_rate * total_k).astype(jnp.bfloat16)
    new_v = (w_value.astype(jnp.float32) - step_rate * total_v).astype(jnp.bfloat16)
    roll_q, roll_k, roll_v = to_rollout(new_q, new_k, new_v)
    return (roll_q, roll_k, roll_v)


def solution(mesh):
    in_specs = (
        P(("section", "dp"), "fsdp", None),
        P(("section", "dp"), None, "fsdp"),
        P(("section", "dp"), None),
        P(("section", "dp"), None),
        P("fsdp", None),
        P("fsdp", None),
        P("fsdp", None),
    )
    out_specs = (P(None, "fsdp"), P(None, "fsdp"), P(None, "fsdp"))
    return jax.shard_map(local, mesh=mesh, in_specs=in_specs, out_specs=out_specs, check_vma=False)
```

profile of v0, /device:TPU:8, one launch (start us, length us, event | category | flops | bytes accessed | tf_op | source)
XLA Modules:
  0.0 846.2 jit_solution(17943018369116252911)
XLA Ops:
  7.2 0.7 all-gather.2.cloned.1.call-update
  7.9 4.1 copy.52
  12.0 13.0 %all-to-all-start.1 = ((bf16[128,64,128]{0,2,1:T(8,128)(2,1)}), bf16[128,64,128]{0,2,1:T(8,128)(2,1)S(1)}, u32[]{:S(2)}, u32[]{:S(2)}) async-start(bf16[128,64,128]{0,2,1:T(8,128)(2,1)} %bitcast.162), calls=%async_computation.1 | async-start | bytes 4194304 | tf_op jit(solution)/shard_map/all_to_all | solution.py:109
  25.2 67.2 %all-to-all-done.1 = bf16[128,64,128]{0,2,1:T(8,128)(2,1)S(1)} async-done(((bf16[128,64,128]{0,2,1:T(8,128)(2,1)}), bf16[128,64,128]{0,2,1:T(8,128)(2,1)S(1)}, u32[]{:S(2)}, u32[]{:S(2)}) %all-to-all-start.1) | async-done | bytes 2097184 | tf_op jit(solution)/shard_map/all_to_all | solution.py:109
  92.4 1.8 broadcast_in_dim.12
  94.3 6.5 all-to-all-start
  101.1 64.8 %all-to-all-done = bf16[128,64,128]{2,0,1:T(8,128)(2,1)} async-done(((bf16[128,64,128]{2,0,1:T(8,128)(2,1)}), bf16[128,64,128]{2,0,1:T(8,128)(2,1)}, u32[]{:S(2)}, u32[]{:S(2)}) %all-to-all-start) | async-done | bytes 2097184 | tf_op jit(solution)/shard_map/all_to_all | solution.py:110
  165.9 1.8 broadcast_in_dim.16
  167.8 8.7 %all-to-all-start.2 = ((bf16[128,64,128]{2,0,1:T(8,128)(2,1)}), bf16[128,64,128]{2,0,1:T(8,128)(2,1)}, u32[]{:S(2)}, u32[]{:S(2)}) async-start(bf16[128,64,128]{2,0,1:T(8,128)(2,1)} %bitcast.158), calls=%async_computation.2 | async-start | bytes 4194304 | tf_op jit(solution)/shard_map/all_to_all | solution.py:111
  176.7 2.9 copy.53
  179.6 161.1 %all-gather.2.cloned.1.call-done = bf16[1,512,8192]{2,1,0:T(8,128)(2,1)} async-done(((bf16[1,8,8192]{2,1,0:T(8,128)(2,1)}), bf16[1,512,8192]{2,1,0:T(8,128)(2,1)}) %all-gather.2.cloned.1.call-update) | async-done | bytes 8388624 | tf_op jit(solution)/shard_map/all_gather | solution.py:114
  340.8 5.3 fusion
  346.5 4.7 fusion.8
  351.2 4.7 fusion.9
  355.9 0.6 fusion.75
  356.6 0.6 copy-done.5
  357.7 8.4 convolution_convert_fusion
  366.2 24.6 %all-to-all-start.7 = ((bf16[64,128,128]{2,1,0:T(8,128)(2,1)}), bf16[64,128,128]{2,1,0:T(8,128)(2,1)S(1)}, u32[]{:S(2)}, u32[]{:S(2)}) async-start(bf16[64,128,128]{2,1,0:T(8,128)(2,1)} %bitcast.165), calls=%async_computation.7 | async-start | bytes 4194304 | tf_op jit(solution)/shard_map/all_to_all | solution.py:162
  390.8 8.2 multiply_reduce_fusion
  399.0 1.5 fusion.16
  400.5 1.1 fusion.7
  402.5 8.1 convolution_convert_fusion.1
  410.6 28.2 %all-to-all-done.7 = bf16[64,128,128]{2,1,0:T(8,128)(2,1)S(1)} async-done(((bf16[64,128,128]{2,1,0:T(8,128)(2,1)}), bf16[64,128,128]{2,1,0:T(8,128)(2,1)S(1)}, u32[]{:S(2)}, u32[]{:S(2)}) %all-to-all-start.7) | async-done | bytes 2097184 | tf_op jit(solution)/shard_map/all_to_all | solution.py:162
  438.8 10.3 %all-to-all-start.5 = ((bf16[64,128,128]{2,1,0:T(8,128)(2,1)}), bf16[64,128,128]{2,1,0:T(8,128)(2,1)}, u32[]{:S(2)}, u32[]{:S(2)}) async-start(bf16[64,128,128]{2,1,0:T(8,128)(2,1)} %bitcast.167), calls=%async_computation.5 | async-start | bytes 4194304 | tf_op jit(solution)/shard_map/all_to_all | solution.py:161
  449.2 8.1 convolution_convert_fusion.2
  457.3 42.5 %all-to-all-done.5 = bf16[64,128,128]{2,1,0:T(8,128)(2,1)} async-done(((bf16[64,128,128]{2,1,0:T(8,128)(2,1)}), bf16[64,128,128]{2,1,0:T(8,128)(2,1)}, u32[]{:S(2)}, u32[]{:S(2)}) %all-to-all-start.5) | async-done | bytes 2097184 | tf_op jit(solution)/shard_map/all_to_all | solution.py:161
  499.8 7.3 all-to-all-start.3
  507.1 2.0 bitcast_reduce_fusion
  509.1 1.0 copy.62
  510.1 2.0 bitcast_reduce_fusion.1
  512.1 1.0 copy.59
  513.1 23.7 %all-to-all-done.3 = bf16[64,128,128]{2,1,0:T(8,128)(2,1)S(1)} async-done(((bf16[64,128,128]{2,1,0:T(8,128)(2,1)}), bf16[64,128,128]{2,1,0:T(8,128)(2,1)S(1)}, u32[]{:S(2)}, u32[]{:S(2)}) %all-to-all-start.3) | async-done | bytes 2097184 | tf_op jit(solution)/shard_map/all_to_all | solution.py:160
  536.8 2.4 copy_bitcast_fusion
  539.4 0.7 copy-done.4
  540.3 110.7 %all-reduce.3.cloned.1.call-done = (f32[128,8192]{1,0:T(8,128)}, f32[128,1024]{0,1:T(8,128)}, f32[128,1024]{0,1:T(8,128)}) async-done(((f32[128,8192]{1,0:T(8,128)}, f32[128,1024]{0,1:T(8,128)}, f32[128,1024]{0,1:T(8,128)}), (f32[128,8192]{1,0:T(8,128)}, f32[128,1024]{0,1:T(8,128)}, f32[128,1024]{0,1:T(8,128)})) %all-reduce.3.cloned.1.call-update) | async-done | bytes 5242896 | tf_op jit(solution)/shard_map/psum | solution.py:172
  651.0 1.3 subtract_convert_fusion.1
  652.5 1.9 broadcast_in_dim.17
  654.3 10.6 %all-to-all-start.6 = ((bf16[128,64,128]{2,0,1:T(8,128)(2,1)}), bf16[128,64,128]{2,0,1:T(8,128)(2,1)S(1)}, u32[]{:S(2)}, u32[]{:S(2)}) async-start(bf16[128,64,128]{2,0,1:T(8,128)(2,1)} %bitcast.160), calls=%async_computation.6 | async-start | bytes 4194304 | tf_op jit(solution)/shard_map/all_to_all | solution.py:110
  665.1 50.7 %all-to-all-done.6 = bf16[128,64,128]{2,0,1:T(8,128)(2,1)S(1)} async-done(((bf16[128,64,128]{2,0,1:T(8,128)(2,1)}), bf16[128,64,128]{2,0,1:T(8,128)(2,1)S(1)}, u32[]{:S(2)}, u32[]{:S(2)}) %all-to-all-start.6) | async-done | bytes 2097184 | tf_op jit(solution)/shard_map/all_to_all | solution.py:110
  715.8 1.8 broadcast_in_dim.18
  717.6 7.3 all-to-all-start.8
  724.9 4.8 copy_bitcast_fusion.1
  729.7 45.2 %all-to-all-done.8 = bf16[128,64,128]{2,0,1:T(8,128)(2,1)} async-done(((bf16[128,64,128]{2,0,1:T(8,128)(2,1)}), bf16[128,64,128]{2,0,1:T(8,128)(2,1)}, u32[]{:S(2)}, u32[]{:S(2)}) %all-to-all-start.8) | async-done | bytes 2097184 | tf_op jit(solution)/shard_map/all_to_all | solution.py:111
  774.9 7.1 all-to-all-start.4
  782.0 49.7 %all-to-all-done.4 = bf16[128,64,128]{2,0,1:T(8,128)(2,1)} async-done(((bf16[128,64,128]{2,0,1:T(8,128)(2,1)}), bf16[128,64,128]{2,0,1:T(8,128)(2,1)}, u32[]{:S(2)}, u32[]{:S(2)}) %all-to-all-start.4) | async-done | bytes 2097184 | tf_op jit(solution)/shard_map/all_to_all | solution.py:109
  831.7 3.0 copy.79
  834.8 1.3 copy.80
  836.1 3.0 copy.81
  (48 shorter events, 3.4 us)
Async XLA Ops:
  7.2 333.6 %all-gather.2.cloned.1.call-start = ((), (), s32[]{:S(2)}) async-start(), calls=%async_computation.9 | async-start | bytes 8519680 | tf_op jit(solution)/shard_map/all_gather | solution.py:114
  7.9 17.2 %copy-start.2 = (bf16[128,1024]{1,0:T(8,128)(2,1)S(1)}, bf16[128,1024]{1,0:T(8,128)(2,1)}, u32[]{:S(2)}) copy-start(bf16[128,1024]{1,0:T(8,128)(2,1)} %param.12) | copy-start | bytes 786436
  12.0 80.4 %all-to-all-start.1 = ((bf16[128,64,128]{0,2,1:T(8,128)(2,1)}), bf16[128,64,128]{0,2,1:T(8,128)(2,1)S(1)}, u32[]{:S(2)}, u32[]{:S(2)}) async-start(bf16[128,64,128]{0,2,1:T(8,128)(2,1)} %bitcast.162), calls=%async_computation.1 | async-start | bytes 4194304 | tf_op jit(solution)/shard_map/all_to_all | solution.py:109
  25.1 75.7 %copy-start.7 = (s32[1,512]{1,0:T(1,128)S(1)}, s32[1,512]{1,0:T(1,128)}, u32[]{:S(2)}) copy-start(s32[1,512]{1,0:T(1,128)} %param.9) | copy-start | bytes 6148
  25.1 75.8 %copy-start.13 = (f32[1,8]{1,0:T(1,128)S(1)}, f32[1,8]{1,0:T(1,128)}, u32[]{:S(2)}) copy-start(f32[1,8]{1,0:T(1,128)} %param.10) | copy-start | bytes 100
  25.1 75.9 %copy-start.3 = (bf16[128,1024]{1,0:T(8,128)(2,1)S(1)}, bf16[128,1024]{1,0:T(8,128)(2,1)}, u32[]{:S(2)}) copy-start(bf16[128,1024]{1,0:T(8,128)(2,1)} %param.13) | copy-start | bytes 786436
  94.3 71.6 %all-to-all-start = ((bf16[128,64,128]{2,0,1:T(8,128)(2,1)}), bf16[128,64,128]{2,0,1:T(8,128)(2,1)}, u32[]{:S(2)}, u32[]{:S(2)}) async-start(bf16[128,64,128]{2,0,1:T(8,128)(2,1)} %bitcast.159), calls=%async_computation | async-start | bytes 4194304 | tf_op jit(solution)/shard_map/all_to_all | solution.py:110
  167.8 198.4 %all-to-all-start.2 = ((bf16[128,64,128]{2,0,1:T(8,128)(2,1)}), bf16[128,64,128]{2,0,1:T(8,128)(2,1)}, u32[]{:S(2)}, u32[]{:S(2)}) async-start(bf16[128,64,128]{2,0,1:T(8,128)(2,1)} %bitcast.158), calls=%async_computation.2 | async-start | bytes 4194304 | tf_op jit(solution)/shard_map/all_to_all | solution.py:111
  176.5 179.5 %copy-start.10 = (f32[64]{0:T(128)}, f32[64]{0:T(128)S(1)}, u32[]{:S(2)}) copy-start(f32[64]{0:T(128)S(1)} %multiply_power_fusion) | copy-start | bytes 772
  340.8 5.8 copy-start
  346.0 11.7 %copy-start.8 = (f32[512]{0:T(512)}, f32[512]{0:T(512)S(1)}, u32[]{:S(2)}) copy-start(f32[512]{0:T(512)S(1)} %add_rsqrt_fusion) | copy-start | bytes 6148
  351.2 6.5 copy-start.12
  356.5 0.6 copy-start.5
  356.5 1.0 copy-start.6
  366.2 72.7 %all-to-all-start.7 = ((bf16[64,128,128]{2,1,0:T(8,128)(2,1)}), bf16[64,128,128]{2,1,0:T(8,128)(2,1)S(1)}, u32[]{:S(2)}, u32[]{:S(2)}) async-start(bf16[64,128,128]{2,1,0:T(8,128)(2,1)} %bitcast.165), calls=%async_computation.7 | async-start | bytes 4194304 | tf_op jit(solution)/shard_map/all_to_all | solution.py:162
  399.0 2.9 copy-start.11
  399.0 3.5 copy-start.9
  438.8 18.4 %copy-start.1 = (bf16[64,128,128]{2,1,0:T(8,128)(2,1)}, bf16[64,128,128]{2,1,0:T(8,128)(2,1)S(1)}, u32[]{:S(2)}) copy-start(bf16[64,128,128]{2,1,0:T(8,128)(2,1)S(1)} %all-to-all-done.7) | copy-start | bytes 6291460
  438.8 60.9 %all-to-all-start.5 = ((bf16[64,128,128]{2,1,0:T(8,128)(2,1)}), bf16[64,128,128]{2,1,0:T(8,128)(2,1)}, u32[]{:S(2)}, u32[]{:S(2)}) async-start(bf16[64,128,128]{2,1,0:T(8,128)(2,1)} %bitcast.167), calls=%async_computation.5 | async-start | bytes 4194304 | tf_op jit(solution)/shard_map/all_to_all | solution.py:161
  499.8 37.0 %all-to-all-start.3 = ((bf16[64,128,128]{2,1,0:T(8,128)(2,1)}), bf16[64,128,128]{2,1,0:T(8,128)(2,1)S(1)}, u32[]{:S(2)}, u32[]{:S(2)}) async-start(bf16[64,128,128]{2,1,0:T(8,128)(2,1)} %bitcast.166), calls=%async_computation.3 | async-start | bytes 4194304 | tf_op jit(solution)/shard_map/all_to_all | solution.py:160
  507.1 143.9 %all-reduce.3.cloned.1.call-start = ((), (), s32[]{:S(2)}) async-start(), calls=%async_computation.10 | async-start | bytes 10485760 | tf_op jit(solution)/shard_map/psum | solution.py:172
  539.2 0.9 copy-start.4
  654.3 61.4 %all-to-all-start.6 = ((bf16[128,64,128]{2,0,1:T(8,128)(2,1)}), bf16[128,64,128]{2,0,1:T(8,128)(2,1)S(1)}, u32[]{:S(2)}, u32[]{:S(2)}) async-start(bf16[128,64,128]{2,0,1:T(8,128)(2,1)} %bitcast.160), calls=%async_computation.6 | async-start | bytes 4194304 | tf_op jit(solution)/shard_map/all_to_all | solution.py:110
  717.6 57.3 %all-to-all-start.8 = ((bf16[128,64,128]{2,0,1:T(8,128)(2,1)}), bf16[128,64,128]{2,0,1:T(8,128)(2,1)}, u32[]{:S(2)}, u32[]{:S(2)}) async-start(bf16[128,64,128]{2,0,1:T(8,128)(2,1)} %bitcast.161), calls=%async_computation.8 | async-start | bytes 4194304 | tf_op jit(solution)/shard_map/all_to_all | solution.py:111
  774.9 56.8 %all-to-all-start.4 = ((bf16[128,64,128]{2,0,1:T(8,128)(2,1)}), bf16[128,64,128]{2,0,1:T(8,128)(2,1)}, u32[]{:S(2)}, u32[]{:S(2)}) async-start(bf16[128,64,128]{2,0,1:T(8,128)(2,1)} %copy_bitcast_fusion.1), calls=%async_computation.4 | async-start | bytes 4194304 | tf_op jit(solution)/shard_map/all_to_all | solution.py:109
Sparse Core Ops, SparseCore 0:
  9.8 330.9 all-gather.1
  539.3 111.5 all-reduce.2
where the time goes:
time: 851 us; the launch traced here: 846 us
  waiting for transfers between devices  645 us (76%)
  starting transfers between devices  95.5 us (11%)
  matrix products  44 us (5%)
  local copies, waits for them, and re-layouts  26.5 us (3%)
  other arithmetic  21.1 us (2%)
  between operations  14.6 us (2%)
    all_gather x1, waiting for transfers between devices, local(): gathered = lax.all_gather(hidden, 'fsdp', axis=1, tiled=True)  161 us
    all_to_all x2, waiting for transfers between devices, to_rollout(): lax.all_to_all(q_part, 'fsdp', split_axis=1, concat_axis=0, tiled=True)  117 us
    all_to_all x2, waiting for transfers between devices, to_rollout(): lax.all_to_all(k_wide, 'fsdp', split_axis=1, concat_axis=0, tiled=True)  116 us
    psum x1, waiting for transfers between devices, local(): lax.psum((query_sum, sum_k, sum_v), ('section', 'dp'))  111 us
    all_to_all x2, waiting for transfers between devices, to_rollout(): lax.all_to_all(v_wide, 'fsdp', split_axis=1, concat_axis=0, tiled=True)  45.2 us
    all_to_all x1, waiting for transfers between devices, local(): lax.all_to_all(part_k, 'fsdp', split_axis=0, concat_axis=1, tiled=True)  42.5 us
    all_to_all x1, waiting for transfers between devices, local(): lax.all_to_all(part_v, 'fsdp', split_axis=0, concat_axis=1, tiled=True)  28.2 us
    all_to_all x1, starting transfers between devices, local(): lax.all_to_all(part_v, 'fsdp', split_axis=0, concat_axis=1, tiled=True)  24.6 us
  transfers between devices with their start and end apart: 11, of which 10 were waited for; matrix products, arithmetic and copies ran while one was open for 9% of the time, Pallas kernels for 0%

commit v1 on v0

v1 whole, which is shorter than its diff:
```python
import jax
import jax.numpy as jnp
from jax import lax
from jax.sharding import Mesh, PartitionSpec as P

D = 8192
HD = 128
RESP = 8

step_rate = 200.0
rope_base = 1000000.0
norm_eps = 1e-06
masked_score = -1e30

YZ = ("y", "zh", "zl")
KH = ("y", "zh")
MEM = ("zl", "core")
X = ("xh", "xl")
FS = ("y", "zh", "zl", "xl")


def rotate(field, cosine_table, sine_table):
    half_width = field.shape[-1] // 2
    lead_half = field[..., :half_width]
    tail_half = field[..., half_width:]
    return jnp.concatenate(
        [
            lead_half * cosine_table - tail_half * sine_table,
            tail_half * cosine_table + lead_half * sine_table,
        ],
        -1,
    )


def angles(seg_row):
    span_count = seg_row.shape[0]
    earlier = jnp.sum((seg_row[None, :] < seg_row[:, None]).astype(jnp.int32), axis=1)
    positions = jnp.arange(span_count, dtype=jnp.int32) - earlier
    frequency = rope_base ** (-jnp.arange(HD // 2, dtype=jnp.float32) * 2.0 / HD)
    phase_grid = positions.astype(jnp.float32)[:, None] * frequency[None, :]
    return jnp.cos(phase_grid), jnp.sin(phase_grid)


def token_weights(seg_row, advantage_row):
    id_range = jnp.arange(RESP + 1, dtype=jnp.int32)
    onehot = (seg_row[:, None] == id_range[None, :]).astype(jnp.float32)
    counts = jnp.sum(onehot, axis=0)[:RESP]
    per_token = -advantage_row / counts
    return jnp.sum(onehot[:, :RESP] * per_token[None, :], axis=1)


def attend_back(q_rot, k_rot, v_bf, grad_context, allowed):
    score_scale = HD ** (-0.5)
    f32 = jnp.float32
    scores = jnp.einsum("td,ud->tu", q_rot, k_rot, preferred_element_type=f32) * score_scale
    scores = jnp.where(allowed, scores, masked_score)
    row_top = jnp.max(scores, axis=-1, keepdims=True)
    exponent = jnp.exp(scores - row_top)
    attention = exponent / jnp.sum(exponent, axis=-1, keepdims=True)
    attention_bf = attention.astype(jnp.bfloat16)
    grad_prob = jnp.einsum("td,ud->tu", grad_context, v_bf, preferred_element_type=f32)
    inner_sum = jnp.sum(attention * grad_prob, axis=-1, keepdims=True)
    dscore = (attention * (grad_prob - inner_sum)).astype(jnp.bfloat16)
    grad_query = jnp.einsum("tu,ud->td", dscore, k_rot, preferred_element_type=f32) * score_scale
    grad_key = jnp.einsum("tu,td->ud", dscore, q_rot, preferred_element_type=f32) * score_scale
    grad_value = jnp.einsum("tu,td->ud", attention_bf, grad_context, preferred_element_type=f32)
    return grad_query, grad_key, grad_value


def swap(x):
    return lax.ppermute(x, ("xl", "core"), [(0, 0), (1, 2), (2, 1), (3, 3)])


def flip(x, axes):
    n = 2 ** len(axes)
    return lax.ppermute(x, axes, [(i, n - 1 - i) for i in range(n)])


def exchange(x, axes):
    return lax.all_to_all(x, axes, split_axis=0, concat_axis=0, tiled=True)


def spread(x, axes):
    n = lax.axis_size(axes)
    return exchange(jnp.broadcast_to(x[None], (n,) + x.shape), axes)


def ordered(mine, other, bit):
    first = jnp.where(bit == 0, mine, other)
    second = jnp.where(bit == 0, other, mine)
    return first, second


def local(hidden, cotangent, seg_ids, advantage, w_query, w_key, w_value):
    f32 = jnp.float32
    bf16 = jnp.bfloat16
    inv_width = D ** (-0.5)
    xh = lax.axis_index("xh")
    xl = lax.axis_index("xl")
    core = lax.axis_index("core")
    zl = lax.axis_index("zl")
    member = zl * 2 + core
    ring = xh * 2 + xl

    token_rows = hidden[0].astype(f32)
    normed_own = (
        token_rows * lax.rsqrt(jnp.mean(token_rows * token_rows, axis=-1, keepdims=True) + norm_eps)
    ).astype(bf16)
    normed_own = swap(normed_own)
    cot = swap(cotangent[0])
    seg_row = swap(seg_ids[0])
    adv_row = swap(advantage[0])
    normed = lax.all_gather(normed_own, YZ + ("core",), axis=0, tiled=True)
    block_len = normed.shape[0]

    wq = w_query.reshape(2, 64, 32, 2, HD)
    wq = lax.dynamic_index_in_dim(wq, xh, 0, keepdims=False)
    wq = lax.dynamic_index_in_dim(wq, core, 2, keepdims=False)
    wq = exchange(wq.transpose(1, 0, 2), YZ)
    wq_l = flip(wq, ("xl",))
    wq_h = flip(wq, ("xh",))
    wq_b = flip(wq, X)
    mine = ordered(wq, wq_l, xl)
    theirs = ordered(wq_h, wq_b, xl)
    row0 = ordered(mine[0], theirs[0], xh)
    row1 = ordered(mine[1], theirs[1], xh)
    q_cols = jnp.stack([row0[0], row0[1], row1[0], row1[1]], axis=1).reshape(D, HD)

    wkv = jnp.concatenate([w_key.reshape(128, 8, HD), w_value.reshape(128, 8, HD)], axis=-1)
    wkv = swap(exchange(wkv.transpose(1, 0, 2), KH))

    cosine_table, sine_table = angles(seg_row)
    weight_row = token_weights(seg_row, adv_row)
    grad_context = (cot.astype(f32) * weight_row[:, None]).astype(bf16)
    place = jnp.arange(block_len, dtype=jnp.int32)
    allowed = (seg_row[:, None] == seg_row[None, :]) & (place[None, :] <= place[:, None])

    normed_m = lax.dynamic_index_in_dim(
        normed.reshape(block_len, 8, 8, HD), member, 2, keepdims=False
    ).reshape(block_len, 1024)
    kv_part = jnp.dot(normed_m, wkv.reshape(1024, 2 * HD), preferred_element_type=f32)
    kv_own = jnp.sum(exchange(kv_part.reshape(8, 64, 2 * HD), MEM), axis=0) * inv_width
    cos_own = lax.dynamic_slice_in_dim(cosine_table, member * 64, 64)
    sin_own = lax.dynamic_slice_in_dim(sine_table, member * 64, 64)
    kv_own = jnp.concatenate(
        [rotate(kv_own[:, :HD], cos_own, sin_own), kv_own[:, HD:]], -1
    ).astype(bf16)
    kv = spread(kv_own, MEM).reshape(block_len, 2 * HD)

    queries = jnp.dot(normed, q_cols, preferred_element_type=f32) * inv_width
    q_rot = rotate(queries, cosine_table, sine_table).astype(bf16)

    grad_query, grad_key, grad_value = attend_back(
        q_rot, kv[:, :HD], kv[:, HD:], grad_context, allowed
    )
    scaled_q = (rotate(grad_query, cosine_table, -sine_table) * inv_width).astype(bf16)
    scaled_kv = (
        jnp.concatenate([rotate(grad_key, cosine_table, -sine_table), grad_value], -1) * inv_width
    ).astype(bf16)
    kv_sum = exchange(scaled_kv.reshape(8, 64, 2 * HD), MEM).astype(f32)
    kv_sum = jnp.sum(kv_sum, axis=0).astype(bf16)
    kv_sum = spread(kv_sum, MEM).reshape(block_len, 2 * HD)

    contract = (((0,), (0,)), ((), ()))
    part_q = lax.dot_general(normed, scaled_q, contract, preferred_element_type=f32).astype(bf16)
    part_q = exchange(part_q.reshape(4, 2048, HD), X).astype(f32)
    old_q = lax.dynamic_slice_in_dim(q_cols, ring * 2048, 2048)
    new_q = (old_q.astype(f32) - step_rate * jnp.sum(part_q, axis=0)).astype(bf16)
    near = swap(new_q)
    far = lax.ppermute(
        new_q,
        ("xh", "xl", "core"),
        [(h * 4 + l * 2 + c, (1 - h) * 4 + c * 2 + l) for h in (0, 1) for l in (0, 1) for c in (0, 1)],
    )
    near_c = flip(near, ("core",))
    far_c = flip(far, ("core",))
    near = ordered(near, near_c, core)
    far = ordered(far, far_c, core)
    low = ordered(near[0], far[0], xh)
    high = ordered(near[1], far[1], xh)
    roll_q = jnp.stack([low[0], high[0], low[1], high[1]], axis=0).reshape(D, HD)

    part_kv = lax.dot_general(normed_m, kv_sum, contract, preferred_element_type=f32).astype(bf16)
    part_kv = exchange(part_kv.reshape(4, 256, 2 * HD), X).astype(f32)
    old_kv = lax.dynamic_slice_in_dim(wkv, ring * 2, 2).reshape(256, 2 * HD)
    new_kv = (old_kv.astype(f32) - step_rate * jnp.sum(part_kv, axis=0)).astype(bf16)
    new_kv = spread(new_kv, ("zl",))
    new_kv = spread(new_kv, X)
    other = flip(new_kv, ("core",))
    new_kv = jnp.stack(ordered(new_kv, other, core), axis=0)
    new_kv = new_kv.reshape(2, 4, 4, 2, 128, 2 * HD).transpose(1, 3, 2, 0, 4, 5).reshape(D, 2 * HD)
    return roll_q, new_kv[:, :HD], new_kv[:, HD:]


def solution(mesh):
    grid = Mesh(
        mesh.devices.reshape(2, 4, 2, 4, 2, 2), ("xh", "y", "zh", "zl", "xl", "core")
    )
    groups = ("xh", "core")
    in_specs = (
        P(groups, FS, None),
        P(groups, None, FS),
        P(groups, None),
        P(groups, None),
        P(FS, None),
        P(FS, None),
        P(FS, None),
    )
    out_specs = (P(None, FS), P(None, FS), P(None, FS))
    return jax.shard_map(local, mesh=grid, in_specs=in_specs, out_specs=out_specs, check_vma=False)
```

time: 851 us -> 326 us (0.38)
  waiting for transfers between devices: 645 us -> 130 us
  blocking collectives: 0 us -> 40.8 us
  starting transfers between devices: 95.5 us -> 63.1 us
  matrix products: 44 us -> 20 us
    all_to_all x9 -> x7, waiting for transfers between devices: 372 us -> 75.5 us  [exchange(): return lax.all_to_all(x, axes, split_axis=0, concat_axis=0, tiled=True)]
    all_gather x1, waiting for transfers between devices: 161 us -> 19.4 us  [local(): normed = lax.all_gather(normed_own, YZ + ('core',), axis=0, tiled=True)]
    psum x1 -> x0, waiting for transfers between devices: 111 us -> none  [local(): lax.psum((query_sum, sum_k, sum_v), ('section', 'dp'))]
    all_to_all x9 -> x7, starting transfers between devices: 95.4 us -> 42.2 us  [exchange(): return lax.all_to_all(x, axes, split_axis=0, concat_axis=0, tiled=True)]
    all_to_all x0 -> x3, blocking collectives: none -> 40.8 us  [exchange(): return lax.all_to_all(x, axes, split_axis=0, concat_axis=0, tiled=True)]
    ppermute x0 -> x13, waiting for transfers between devices: none -> 34.9 us  [the longest x6 22.5 us: flip(): return lax.ppermute(x, axes, [(i, n - 1 - i) for i in range(n)])]
    dot_general x9, matrix products: 44 us -> 20 us  [the longest x1 7.11 us: local(): lax.dot_general(normed, scaled_q, contract, preferred_element_type=f32)]
    ppermute x0 -> x13, starting transfers between devices: none -> 20.9 us  [the longest x6 12.3 us: flip(): return lax.ppermute(x, axes, [(i, n - 1 - i) for i in range(n)])]
  transfers between devices with their start and end apart: 11 -> 21, of which waited for: 10 -> 13; matrix products, arithmetic and copies ran while one was open for 9% -> 16% of each run, Pallas kernels for 0% -> 0%
where the time goes in v1:
time: 326 us; the launch traced here: 322 us
  waiting for transfers between devices  130 us (40%)
  starting transfers between devices  63.1 us (19%)
  blocking collectives  40.8 us (13%)
  local copies, waits for them, and re-layouts  32.5 us (10%)
  other arithmetic  20.9 us (6%)
  matrix products  20 us (6%)
  between operations  14.5 us (4%)
    all_to_all x7, waiting for transfers between devices, exchange(): return lax.all_to_all(x, axes, split_axis=0, concat_axis=0, tiled=True)  75.5 us
    all_to_all x7, starting transfers between devices, exchange(): return lax.all_to_all(x, axes, split_axis=0, concat_axis=0, tiled=True)  42.2 us
    all_to_all x3, blocking collectives, exchange(): return lax.all_to_all(x, axes, split_axis=0, concat_axis=0, tiled=True)  40.8 us
    ppermute x6, waiting for transfers between devices, flip(): return lax.ppermute(x, axes, [(i, n - 1 - i) for i in range(n)])  22.5 us
    all_gather x1, waiting for transfers between devices, local(): normed = lax.all_gather(normed_own, YZ + ('core',), axis=0, tiled=True)  19.4 us
    ppermute x1, waiting for transfers between devices, local(): lax.ppermute(new_q, ('xh', 'xl', 'core'), [(h * 4 + l * 2 + c, (1 - h) *...  12.3 us
    ppermute x6, starting transfers between devices, flip(): return lax.ppermute(x, axes, [(i, n - 1 - i) for i in range(n)])  12.3 us
    unnamed x30, local copies, waits for them, and re-layouts  10.7 us
  transfers between devices with their start and end apart: 21, of which 13 were waited for; matrix products, arithmetic and copies ran while one was open for 16% of the time, Pallas kernels for 0%

profile of v1, /device:TPU:8, one launch (start us, length us, event | category | flops | bytes accessed | tf_op | source)
XLA Modules:
  0.0 321.7 jit_solution(6756234446904016995)
XLA Ops:
  10.7 3.2 %reshape.127 = bf16[2,64,32,2,128]{4,3,2,1,0:T(2,128)(2,1)S(1)} reshape(bf16[128,8192]{1,0:T(8,128)(2,1)} %param.11) | data formatting | bytes 4194304 | tf_op jit(solution)/shard_map/reshape | solution.py:116
  14.0 1.2 constant_dynamic-slice_fusion.2
  15.2 1.4 copy.73
  16.6 11.8 %all-to-all-start = ((bf16[32,64,128]{2,1,0:T(8,128)(2,1)}), bf16[32,64,128]{2,1,0:T(8,128)(2,1)S(1)}, u32[]{:S(2)}, u32[]{:S(2)}) async-start(bf16[32,64,128]{2,1,0:T(8,128)(2,1)} %bitcast.87), calls=%async_computation | async-start | bytes 1048576 | tf_op jit(solution)/shard_map/all_to_all | solution.py:80
  29.5 12.1 %all-to-all-done = bf16[32,64,128]{2,1,0:T(8,128)(2,1)S(1)} async-done(((bf16[32,64,128]{2,1,0:T(8,128)(2,1)}), bf16[32,64,128]{2,1,0:T(8,128)(2,1)S(1)}, u32[]{:S(2)}, u32[]{:S(2)}) %all-to-all-start) | async-done | bytes 524320 | tf_op jit(solution)/shard_map/all_to_all | solution.py:80
  41.6 9.5 %all-to-all-start.1 = ((bf16[8,128,256]{2,1,0:T(8,128)(2,1)}), bf16[8,128,256]{2,1,0:T(8,128)(2,1)}, u32[]{:S(2)}, u32[]{:S(2)}) async-start(bf16[8,128,256]{2,1,0:T(8,128)(2,1)} %maximum_bitcast_fusion.1), calls=%async_computation.1 | async-start | bytes 1048576 | tf_op jit(solution)/shard_map/all_to_all | solution.py:80
  51.8 1.8 collective-permute-start.7
  53.6 7.3 %collective-permute-start = (bf16[32,64,128]{2,1,0:T(8,128)(2,1)S(1)}, bf16[32,64,128]{2,1,0:T(8,128)(2,1)S(1)}, u32[]{:S(2)}, u32[]{:S(2)}) collective-permute-start(bf16[32,64,128]{2,1,0:T(8,128)(2,1)S(1)} %all-to-all-done), channel_id=1, source_target_pairs={{0,2},{2,0},{1,3},{3,1},{4,6},{6,4},{5,7},{7,5},{8,10},{10,8},{9,1... | collective-permute-start | bytes 1572872 | tf_op jit(solution)/shard_map/ppermute | solution.py:76
  61.0 2.8 collective-permute-start.1
  63.8 2.2 collective-permute-start.6
  66.3 7.4 %collective-permute-done = bf16[32,64,128]{2,1,0:T(8,128)(2,1)S(1)} collective-permute-done((bf16[32,64,128]{2,1,0:T(8,128)(2,1)S(1)}, bf16[32,64,128]{2,1,0:T(8,128)(2,1)S(1)}, u32[]{:S(2)}, u32[]{:S(2)}) %collective-permute-start) | collective-permute-done | bytes 524320 | tf_op jit(solution)/shard_map/ppermute | solution.py:76
  73.8 1.7 collective-permute-start.5
  75.4 12.4 %collective-permute-done.1 = bf16[32,64,128]{2,1,0:T(8,128)(2,1)S(1)} collective-permute-done((bf16[32,64,128]{2,1,0:T(8,128)(2,1)S(1)}, bf16[32,64,128]{2,1,0:T(8,128)(2,1)S(1)}, u32[]{:S(2)}, u32[]{:S(2)}) %collective-permute-start.1) | collective-permute-done | bytes 524320 | tf_op jit(solution)/shard_map/ppermute | solution.py:76
  88.3 1.6 select_bitcast_fusion.7
  89.9 19.4 %all-gather.2.cloned.1.call-done = bf16[512,8192]{1,0:T(8,128)(2,1)} async-done(((bf16[8,8192]{1,0:T(8,128)(2,1)}), bf16[512,8192]{1,0:T(8,128)(2,1)}) %all-gather.2.cloned.1.call-update) | async-done | bytes 8388624 | tf_op jit(solution)/shard_map/all_gather | solution.py:113
  109.3 9.3 %copy.64 = bf16[64,8,64,128]{3,2,1,0:T(8,128)(2,1)} copy(bf16[64,8,64,128]{3,1,2,0:T(8,128)(2,1)} %bitcast.88) | data formatting | bytes 16777216
  118.6 5.6 %constant_dynamic-slice_fusion.1 = bf16[512,8,1,128]{3,2,1,0:T(2,128)(2,1)S(1)} fusion(bf16[512,8,8,128]{3,2,1,0:T(8,128)(2,1)} %bitcast.90, s32[]{:T(128)S(6)} %select_n.135), kind=kLoop, calls=%fused_computation.100 | loop fusion | bytes 2097156 | tf_op jit(solution)/shard_map/jit(dynamic_index_in_dim)/dynamic_slice | solution.py:138
  124.9 1.2 fusion.50
  126.1 4.3 %all-to-all-start.2 = ((f32[8,64,256]{2,1,0:T(8,128)}), f32[8,64,256]{2,1,0:T(8,128)}, u32[]{:S(2)}, u32[]{:S(2)}) async-start(f32[8,64,256]{2,1,0:T(8,128)} %fusion.50), calls=%async_computation.2 | async-start | bytes 1048576 | tf_op jit(solution)/shard_map/all_to_all | solution.py:80
  130.4 1.8 pad_maximum_fusion
  132.2 6.3 %convolution_multiply_fusion.3 = f32[512,128]{0,1:T(8,128)S(1)} fusion(bf16[512,8192]{1,0:T(8,128)(2,1)} %all-gather.2.cloned.1.call-done, bf16[8192,128]{1,0:T(8,128)(2,1)S(1)} %bitcast.91), kind=kOutput, calls=%fused_computation.11 | convolution fusion | flops 1073807360 | bytes 10747904 | tf_op jit(solution)/shard_map/dot_general | solution.py:150
  138.5 1.3 fusion.32
  139.8 5.8 %all-to-all-done.2 = f32[8,64,256]{2,1,0:T(8,128)} async-done(((f32[8,64,256]{2,1,0:T(8,128)}), f32[8,64,256]{2,1,0:T(8,128)}, u32[]{:S(2)}, u32[]{:S(2)}) %all-to-all-start.2) | async-done | bytes 524320 | tf_op jit(solution)/shard_map/all_to_all | solution.py:80
  148.5 3.4 %all-to-all-start.3 = ((bf16[8,64,256]{2,1,0:T(8,128)(2,1)}), bf16[8,64,256]{2,1,0:T(8,128)(2,1)S(1)}, u32[]{:S(2)}, u32[]{:S(2)}) async-start(bf16[8,64,256]{2,1,0:T(8,128)(2,1)} %broadcast_in_dim.11), calls=%async_computation.3 | async-start | bytes 524288 | tf_op jit(solution)/shard_map/all_to_all | solution.py:80
  153.2 8.3 %all-to-all-done.3 = bf16[8,64,256]{2,1,0:T(8,128)(2,1)S(1)} async-done(((bf16[8,64,256]{2,1,0:T(8,128)(2,1)}), bf16[8,64,256]{2,1,0:T(8,128)(2,1)S(1)}, u32[]{:S(2)}, u32[]{:S(2)}) %all-to-all-start.3) | async-done | bytes 262176 | tf_op jit(solution)/shard_map/all_to_all | solution.py:80
  162.3 1.4 multiply_reduce_fusion
  165.2 1.3 fusion.29
  167.6 1.7 copy.58
  169.3 1.8 fusion.8
  171.4 12.1 %all_to_all.50 = bf16[8,64,256]{2,1,0:T(8,128)(2,1)S(1)} all-to-all(bf16[8,64,256]{2,1,0:T(8,128)(2,1)S(1)} %fusion.7), channel_id=1, replica_groups=mesh['xh'=2,'y'=4,'zh'=2,'zl'=4,'xl'=2,'core'=2] {'zl','core'}, dimensions={0} | all-to-all | bytes 524288 | tf_op jit(solution)/shard_map/all_to_all | solution.py:80
  184.9 12.1 %all_to_all.51 = bf16[8,64,256]{2,1,0:T(8,128)(2,1)S(1)} all-to-all(bf16[8,64,256]{2,1,0:T(8,128)(2,1)S(1)} %broadcast_in_dim.13), channel_id=1, replica_groups=mesh['xh'=2,'y'=4,'zh'=2,'zl'=4,'xl'=2,'core'=2] {'zl','core'}, dimensions={0} | all-to-all | bytes 524288 | tf_op jit(solution)/shard_map/all_to_all | solution.py:80
  197.0 1.3 convolution_convert_fusion.1
  198.4 4.2 %all-to-all-start.7 = ((bf16[4,256,256]{2,1,0:T(8,128)(2,1)}), bf16[4,256,256]{2,1,0:T(8,128)(2,1)S(1)}, u32[]{:S(2)}, u32[]{:S(2)}) async-start(bf16[4,256,256]{2,1,0:T(8,128)(2,1)} %bitcast.103), calls=%async_computation.7 | async-start | bytes 1048576 | tf_op jit(solution)/shard_map/all_to_all | solution.py:80
  202.6 7.1 %convolution_convert_fusion = bf16[8192,128]{1,0:T(8,128)(2,1)} fusion(bf16[512,8192]{1,0:T(8,128)(2,1)} %all-gather.2.cloned.1.call-done, f32[512,64]{0,1:T(8,128)S(1)} %get-tuple-element.23, f32[512,64]{0,1:T(8,128)S(1)} %copy-done.7), kind=kOutput, calls=%fused_computation | convolution fusion | flops 1074987008 | bytes 10747904 | tf_op jit(solution)/shard_map/dot_general | solution.py:165
  209.7 2.0 all-to-all-done.7
  211.7 4.5 %all-to-all-start.4 = ((bf16[4,2048,128]{2,1,0:T(8,128)(2,1)}), bf16[4,2048,128]{2,1,0:T(8,128)(2,1)}, u32[]{:S(2)}, u32[]{:S(2)}) async-start(bf16[4,2048,128]{2,1,0:T(8,128)(2,1)} %bitcast.18), calls=%async_computation.4 | async-start | bytes 4194304 | tf_op jit(solution)/shard_map/all_to_all | solution.py:80
  217.2 23.8 %all-to-all-done.4 = bf16[4,2048,128]{2,1,0:T(8,128)(2,1)} async-done(((bf16[4,2048,128]{2,1,0:T(8,128)(2,1)}), bf16[4,2048,128]{2,1,0:T(8,128)(2,1)}, u32[]{:S(2)}, u32[]{:S(2)}) %all-to-all-start.4) | async-done | bytes 2097184 | tf_op jit(solution)/shard_map/all_to_all | solution.py:80
  241.1 16.6 %all_to_all.52 = bf16[4,256,256]{2,1,0:T(8,128)(2,1)S(1)} all-to-all(bf16[4,256,256]{2,1,0:T(8,128)(2,1)S(1)} %broadcast_in_dim.14), channel_id=1, replica_groups=mesh['xh'=2,'y'=4,'zh'=2,'zl'=4,'xl'=2,'core'=2] {'zl'}, dimensions={0} | all-to-all | bytes 1048576 | tf_op jit(solution)/shard_map/all_to_all | solution.py:80
  257.7 1.5 broadcast_in_dim.15
  259.2 4.4 %all-to-all-start.9 = ((bf16[4,4,256,256]{3,2,1,0:T(8,128)(2,1)}), bf16[4,4,256,256]{3,2,1,0:T(8,128)(2,1)}, u32[]{:S(2)}, u32[]{:S(2)}) async-start(bf16[4,4,256,256]{3,2,1,0:T(8,128)(2,1)} %broadcast_in_dim.15), calls=%async_computation.9 | async-start | bytes 4194304 | tf_op jit(solution)/shard_map/all_to_all | solution.py:80
  263.6 2.0 convert_reduce_fusion
  265.6 23.4 %all-to-all-done.9 = bf16[4,4,256,256]{3,2,1,0:T(8,128)(2,1)} async-done(((bf16[4,4,256,256]{3,2,1,0:T(8,128)(2,1)}), bf16[4,4,256,256]{3,2,1,0:T(8,128)(2,1)}, u32[]{:S(2)}, u32[]{:S(2)}) %all-to-all-start.9) | async-done | bytes 2097184 | tf_op jit(solution)/shard_map/all_to_all | solution.py:80
  290.7 12.3 %collective-permute-done.10 = bf16[2048,128]{1,0:T(8,128)(2,1)S(1)} collective-permute-done((bf16[2048,128]{1,0:T(8,128)(2,1)S(1)}, bf16[2048,128]{1,0:T(8,128)(2,1)S(1)}, u32[]{:S(2)}, u32[]{:S(2)}) %collective-permute-start.10) | collective-permute-done | bytes 524320 | tf_op jit(solution)/shard_map/ppermute | solution.py:170
  303.0 2.1 collective-permute-start.11
  305.2 1.5 collective-permute-done.11
  307.6 1.6 pad_maximum_fusion.1
  309.2 2.5 broadcast_select_fusion.1
  312.6 2.3 fusion.49
  (86 shorter events, 20.1 us)
Async XLA Ops:
  7.2 21.3 %copy-start = (bf16[128,1024]{1,0:T(8,128)(2,1)S(1)}, bf16[128,1024]{1,0:T(8,128)(2,1)}, u32[]{:S(2)}) copy-start(bf16[128,1024]{1,0:T(8,128)(2,1)} %param.12) | copy-start | bytes 786436
  7.2 102.1 %all-gather.2.cloned.1.call-start = ((), (), s32[]{:S(2)}) async-start(), calls=%async_computation.10 | async-start | bytes 8519680 | tf_op jit(solution)/shard_map/all_gather | solution.py:113
  9.4 0.7 collective-permute-start.3
  10.0 0.7 copy-start.9
  14.0 14.5 %copy-start.8 = (bf16[128,1024]{1,0:T(8,128)(2,1)S(1)}, bf16[128,1024]{1,0:T(8,128)(2,1)}, u32[]{:S(2)}) copy-start(bf16[128,1024]{1,0:T(8,128)(2,1)} %param.13) | copy-start | bytes 786436
  16.6 34.5 %copy-start.13 = (s32[1,512]{1,0:T(1,128)S(1)}, s32[1,512]{1,0:T(1,128)}, u32[]{:S(2)}) copy-start(s32[1,512]{1,0:T(1,128)} %param.9) | copy-start | bytes 6148
  16.6 25.0 %all-to-all-start = ((bf16[32,64,128]{2,1,0:T(8,128)(2,1)}), bf16[32,64,128]{2,1,0:T(8,128)(2,1)S(1)}, u32[]{:S(2)}, u32[]{:S(2)}) async-start(bf16[32,64,128]{2,1,0:T(8,128)(2,1)} %bitcast.87), calls=%async_computation | async-start | bytes 1048576 | tf_op jit(solution)/shard_map/all_to_all | solution.py:80
  41.6 24.7 %all-to-all-start.1 = ((bf16[8,128,256]{2,1,0:T(8,128)(2,1)}), bf16[8,128,256]{2,1,0:T(8,128)(2,1)}, u32[]{:S(2)}, u32[]{:S(2)}) async-start(bf16[8,128,256]{2,1,0:T(8,128)(2,1)} %maximum_bitcast_fusion.1), calls=%async_computation.1 | async-start | bytes 1048576 | tf_op jit(solution)/shard_map/all_to_all | solution.py:80
  51.1 12.7 %collective-permute-start.4 = (s32[512]{0:T(512)S(1)}, s32[512]{0:T(512)S(1)}, u32[]{:S(2)}, u32[]{:S(2)}) collective-permute-start(s32[512]{0:T(512)S(1)} %bitcast.106), channel_id=1, source_target_pairs={{0,0},{1,2},{2,1},{3,3},{4,4},{5,6},{6,5},{7,7},{8,8},{9,10},{10,9... | collective-permute-start | bytes 6152 | tf_op jit(solution)/shard_map/ppermute | solution.py:71
  51.8 100.1 %collective-permute-start.7 = (f32[8]{0:T(128)}, f32[8]{0:T(128)}, u32[]{:S(2)}, u32[]{:S(2)}) collective-permute-start(f32[8]{0:T(128)} %bitcast.17), channel_id=1, source_target_pairs={{0,0},{1,2},{2,1},{3,3},{4,4},{5,6},{6,5},{7,7},{8,8},{9,10},{10,9... | collective-permute-start | bytes 104 | tf_op jit(solution)/shard_map/ppermute | solution.py:71
  53.6 20.1 %collective-permute-start = (bf16[32,64,128]{2,1,0:T(8,128)(2,1)S(1)}, bf16[32,64,128]{2,1,0:T(8,128)(2,1)S(1)}, u32[]{:S(2)}, u32[]{:S(2)}) collective-permute-start(bf16[32,64,128]{2,1,0:T(8,128)(2,1)S(1)} %all-to-all-done), channel_id=1, source_target_pairs={{0,2},{2,0},{1,3},{3,1},{4,6},{6,4},{5,7},{7,5},{8,10},{10,8},{9,1... | collective-permute-start | bytes 1572872 | tf_op jit(solution)/shard_map/ppermute | solution.py:76
  61.0 26.9 %collective-permute-start.1 = (bf16[32,64,128]{2,1,0:T(8,128)(2,1)S(1)}, bf16[32,64,128]{2,1,0:T(8,128)(2,1)S(1)}, u32[]{:S(2)}, u32[]{:S(2)}) collective-permute-start(bf16[32,64,128]{2,1,0:T(8,128)(2,1)S(1)} %all-to-all-done), channel_id=1, source_target_pairs={{0,128},{128,0},{1,129},{129,1},{2,130},{130,2},{3,131},{131,3},{4... | collective-permute-start | bytes 1572872 | tf_op jit(solution)/shard_map/ppermute | solution.py:76
  63.8 24.5 %collective-permute-start.2 = (bf16[32,64,128]{2,1,0:T(8,128)(2,1)S(1)}, bf16[32,64,128]{2,1,0:T(8,128)(2,1)S(1)}, u32[]{:S(2)}, u32[]{:S(2)}) collective-permute-start(bf16[32,64,128]{2,1,0:T(8,128)(2,1)S(1)} %all-to-all-done), channel_id=1, source_target_pairs={{0,130},{2,128},{128,2},{130,0},{1,131},{3,129},{129,3},{131,1},{4... | collective-permute-start | bytes 1572872 | tf_op jit(solution)/shard_map/ppermute | solution.py:76
  63.8 74.7 %copy-start.11 = (f32[64]{0:T(128)}, f32[64]{0:T(128)S(1)}, u32[]{:S(2)}) copy-start(f32[64]{0:T(128)S(1)} %multiply_power_fusion) | copy-start | bytes 772
  63.8 98.4 %collective-permute-start.6 = (bf16[512,128]{1,0:T(8,128)(2,1)}, bf16[512,128]{1,0:T(8,128)(2,1)}, u32[]{:S(2)}, u32[]{:S(2)}) collective-permute-start(bf16[512,128]{1,0:T(8,128)(2,1)} %bitcast.16), channel_id=1, source_target_pairs={{0,0},{1,2},{2,1},{3,3},{4,4},{5,6},{6,5},{7,7},{8,8},{9,10},{10,9... | collective-permute-start | bytes 393224 | tf_op jit(solution)/shard_map/ppermute | solution.py:71
  73.8 51.1 %collective-permute-start.5 = (bf16[8,128,256]{2,1,0:T(8,128)(2,1)}, bf16[8,128,256]{2,1,0:T(8,128)(2,1)S(1)}, u32[]{:S(2)}, u32[]{:S(2)}) collective-permute-start(bf16[8,128,256]{2,1,0:T(8,128)(2,1)} %all-to-all-done.1), channel_id=1, source_target_pairs={{0,0},{1,2},{2,1},{3,3},{4,4},{5,6},{6,5},{7,7},{8,8},{9,10},{10,9... | collective-permute-start | bytes 1572872 | tf_op jit(solution)/shard_map/ppermute | solution.py:71
  124.9 5.6 %copy-start.4 = (bf16[8,128,256]{2,1,0:T(8,128)(2,1)}, bf16[8,128,256]{2,1,0:T(8,128)(2,1)S(1)}, u32[]{:S(2)}) copy-start(bf16[8,128,256]{2,1,0:T(8,128)(2,1)S(1)} %collective-permute-done.5) | copy-start | bytes 1572868
  126.1 19.5 %all-to-all-start.2 = ((f32[8,64,256]{2,1,0:T(8,128)}), f32[8,64,256]{2,1,0:T(8,128)}, u32[]{:S(2)}, u32[]{:S(2)}) async-start(f32[8,64,256]{2,1,0:T(8,128)} %fusion.50), calls=%async_computation.2 | async-start | bytes 1048576 | tf_op jit(solution)/shard_map/all_to_all | solution.py:80
  148.5 13.1 %all-to-all-start.3 = ((bf16[8,64,256]{2,1,0:T(8,128)(2,1)}), bf16[8,64,256]{2,1,0:T(8,128)(2,1)S(1)}, u32[]{:S(2)}, u32[]{:S(2)}) async-start(bf16[8,64,256]{2,1,0:T(8,128)(2,1)} %broadcast_in_dim.11), calls=%async_computation.3 | async-start | bytes 524288 | tf_op jit(solution)/shard_map/all_to_all | solution.py:80
  161.6 2.1 copy-start.5
  161.6 0.7 copy-start.10
  161.9 1.8 copy-start.2
  163.7 1.0 copy-start.6
  163.7 1.5 copy-start.12
  169.3 1.8 copy-start.3
  197.0 5.6 %copy-start.7 = (f32[512,64]{0,1:T(8,128)S(1)}, f32[512,64]{0,1:T(8,128)}, u32[]{:S(2)}) copy-start(f32[512,64]{0,1:T(8,128)} %get-tuple-element.24) | copy-start | bytes 393220
  198.4 13.4 %all-to-all-start.7 = ((bf16[4,256,256]{2,1,0:T(8,128)(2,1)}), bf16[4,256,256]{2,1,0:T(8,128)(2,1)S(1)}, u32[]{:S(2)}, u32[]{:S(2)}) async-start(bf16[4,256,256]{2,1,0:T(8,128)(2,1)} %bitcast.103), calls=%async_computation.7 | async-start | bytes 1048576 | tf_op jit(solution)/shard_map/all_to_all | solution.py:80
  211.7 29.3 %all-to-all-start.4 = ((bf16[4,2048,128]{2,1,0:T(8,128)(2,1)}), bf16[4,2048,128]{2,1,0:T(8,128)(2,1)}, u32[]{:S(2)}, u32[]{:S(2)}) async-start(bf16[4,2048,128]{2,1,0:T(8,128)(2,1)} %bitcast.18), calls=%async_computation.4 | async-start | bytes 4194304 | tf_op jit(solution)/shard_map/all_to_all | solution.py:80
  259.2 29.8 %all-to-all-start.9 = ((bf16[4,4,256,256]{3,2,1,0:T(8,128)(2,1)}), bf16[4,4,256,256]{3,2,1,0:T(8,128)(2,1)}, u32[]{:S(2)}, u32[]{:S(2)}) async-start(bf16[4,4,256,256]{3,2,1,0:T(8,128)(2,1)} %broadcast_in_dim.15), calls=%async_computation.9 | async-start | bytes 4194304 | tf_op jit(solution)/shard_map/all_to_all | solution.py:80
  289.0 20.2 %collective-permute-start.12 = (bf16[4,4,256,256]{3,2,1,0:T(8,128)(2,1)}, bf16[4,4,256,256]{3,2,1,0:T(8,128)(2,1)}, u32[]{:S(2)}, u32[]{:S(2)}) collective-permute-start(bf16[4,4,256,256]{3,2,1,0:T(8,128)(2,1)} %all-to-all-done.9), channel_id=1, source_target_pairs={{0,1},{1,0},{2,3},{3,2},{4,5},{5,4},{6,7},{7,6},{8,9},{9,8},{10,11... | collective-permute-start | bytes 6291464 | tf_op jit(solution)/shard_map/ppermute | solution.py:76
  289.1 13.9 %collective-permute-start.10 = (bf16[2048,128]{1,0:T(8,128)(2,1)S(1)}, bf16[2048,128]{1,0:T(8,128)(2,1)S(1)}, u32[]{:S(2)}, u32[]{:S(2)}) collective-permute-start(bf16[2048,128]{1,0:T(8,128)(2,1)S(1)} %subtract_convert_fusion), channel_id=1, source_target_pairs={{0,128},{1,130},{2,129},{3,131},{128,0},{129,2},{130,1},{131,3},{4... | collective-permute-start | bytes 1572872 | tf_op jit(solution)/shard_map/ppermute | solution.py:170
  289.8 15.4 %collective-permute-start.8 = (bf16[2048,128]{1,0:T(8,128)(2,1)S(1)}, bf16[2048,128]{1,0:T(8,128)(2,1)S(1)}, u32[]{:S(2)}, u32[]{:S(2)}) collective-permute-start(bf16[2048,128]{1,0:T(8,128)(2,1)S(1)} %subtract_convert_fusion), channel_id=1, source_target_pairs={{0,0},{1,2},{2,1},{3,3},{4,4},{5,6},{6,5},{7,7},{8,8},{9,10},{10,9... | collective-permute-start | bytes 1572872 | tf_op jit(solution)/shard_map/ppermute | solution.py:71
  303.0 3.7 %collective-permute-start.11 = (bf16[2048,128]{1,0:T(8,128)(2,1)S(1)}, bf16[2048,128]{1,0:T(8,128)(2,1)S(1)}, u32[]{:S(2)}, u32[]{:S(2)}) collective-permute-start(bf16[2048,128]{1,0:T(8,128)(2,1)S(1)} %collective-permute-done.10), channel_id=1, source_target_pairs={{0,1},{1,0},{2,3},{3,2},{4,5},{5,4},{6,7},{7,6},{8,9},{9,8},{10,11... | collective-permute-start | bytes 1572872 | tf_op jit(solution)/shard_map/ppermute | solution.py:76
  305.2 2.3 collective-permute-start.9
  312.6 2.3 copy-start.1
Sparse Core Ops, SparseCore 0:
  10.8 98.4 all-gather.1
